TPU v7x, 32 devices: a whole 2x2x4 slice. The times are simulated.
32 devices in a mesh: section: 2 (over y), expert: 16 (over z, x, core).
Axes of the slice: x: 2, y: 2, z: 4, core: 2. Of those that a mesh axis runs over, the one named last changes fastest.
Arguments:
- forward_input: bfloat16 [128, 3584], P('expert', 'section'), may hold values from -6 to 6
- forward_route: int32 [128, 8], P('expert'), may hold values from 0 to 15, all different within a row; in each aligned block of 8 rows (0 to 7, 8 to 15, ...) at most 8 rows name the same one
- forward_weight: float32 [128, 8], P('expert'), may hold values from 0.05 to 0.5
- output_grad: bfloat16 [128, 3584], P('expert', 'section'), may hold values from -6 to 6
- backward_route: int32 [128, 8], P('expert'), may hold values from 0 to 15, all different within a row; in each aligned block of 8 rows (0 to 7, 8 to 15, ...) at most 8 rows name the same one
- backward_weight: float32 [128, 8], P('expert'), may hold values from 0.05 to 0.5
- gate_stash: bfloat16 [16, 128, 2560], P('expert', None, 'section'), may hold values from -6 to 6
- up_stash: bfloat16 [16, 128, 2560], P('expert', None, 'section'), may hold values from -6 to 6
- gate_matrix: bfloat16 [16, 2560, 3584], P('expert', 'section'), may hold values from -0.125 to 0.125
- up_matrix: bfloat16 [16, 2560, 3584], P('expert', 'section'), may hold values from -0.125 to 0.125
- down_matrix: bfloat16 [16, 2560, 3584], P('expert', 'section'), may hold values from -0.15625 to 0.15625
Outputs:
- forward_output: bfloat16 [128, 3584], P('expert', 'section')
- input_grad: bfloat16 [128, 3584], P('expert', 'section')
Inputs may be any that keep to these rules, and one draw needn't show every extreme that they name: `forward_route`: each row names 8 different experts. In each aligned block of 8 rows (the rows of one index of expert) no expert is named by more than 8 rows, a bound that some block reaches. `backward_route`: as for forward_route.
All inputs are finite; a program needn't handle non-finite values.
Results may differ from a plain program's by a relative error of at most 0.0072.
Values may be sent and summed in bfloat16 or wider, within the bound.
No kernel may reach another device: no remote copies, remote signals or barrier semaphores. Data moves between devices by JAX's collectives and lax.ppermute only.
A program may use at most 128 MiB of HBM per device.

v0:
```python
import jax
import jax.numpy as jnp
from jax import lax
from jax.sharding import PartitionSpec as P


def slot_columns(routes, expert_count, capacity):
    chosen = (
        routes[:, :, None] == jnp.arange(expert_count, dtype=jnp.int32)[None, None, :]
    ).astype(jnp.int32)
    per_token = jnp.sum(chosen, axis=1, dtype=jnp.int32)
    earlier = jnp.cumsum(per_token, axis=0, dtype=jnp.int32) - per_token
    position = jnp.sum(chosen * earlier[:, None, :], axis=2, dtype=jnp.int32)
    return routes * capacity + position


def placement_matrix(columns, weights, total_cols):
    matches = (
        columns[:, :, None] == jnp.arange(total_cols, dtype=jnp.int32)[None, None, :]
    ).astype(jnp.float32)
    return jnp.sum(matches * weights[:, :, None], axis=1)


def contract_last(first_operand, second_operand):
    return lax.dot_general(
        first_operand, second_operand, (((1,), (1,)), ((), ())), preferred_element_type=jnp.float32
    )


def contract_first(first_operand, second_operand):
    return lax.dot_general(
        first_operand, second_operand, (((0,), (1,)), ((), ())), preferred_element_type=jnp.float32
    )


def combine_rows(mixing, returned):
    return lax.dot_general(
        mixing,
        returned.astype(jnp.float32),
        (((1,), (1,)), ((), ())),
        precision=lax.Precision.HIGHEST,
        preferred_element_type=jnp.float32,
    )


def shards(
    forward_input,
    forward_route,
    forward_weight,
    output_grad,
    backward_route,
    backward_weight,
    gate_stash,
    up_stash,
    gate_matrix,
    up_matrix,
    down_matrix,
):
    expert_count = lax.axis_size("expert")
    slot_rows = gate_stash.shape[1]
    capacity = slot_rows // expert_count
    feature_cols = forward_input.shape[1]
    gate_weights = gate_matrix[0]
    up_weights = up_matrix[0]
    down_weights = down_matrix[0]
    unit_weight = jnp.ones(forward_weight.shape, jnp.float32)
    forward_cols = slot_columns(forward_route, expert_count, capacity)
    forward_select = placement_matrix(forward_cols, unit_weight, slot_rows)
    forward_mix = placement_matrix(forward_cols, forward_weight, slot_rows)
    backward_cols = slot_columns(backward_route, expert_count, capacity)
    backward_select = placement_matrix(backward_cols, unit_weight, slot_rows)
    backward_mix = placement_matrix(backward_cols, backward_weight, slot_rows)
    select_rows = forward_select.T.astype(jnp.bfloat16)
    sent = jnp.dot(select_rows, forward_input, preferred_element_type=jnp.float32).astype(
        jnp.bfloat16
    )
    arrived = lax.all_to_all(
        sent.reshape(expert_count, capacity, feature_cols),
        "expert",
        split_axis=0,
        concat_axis=0,
        tiled=True,
    )
    arrived = arrived.reshape(slot_rows, feature_cols)
    portion = lax.all_gather(arrived, "section", axis=1, tiled=True)
    gate_part = gate_weights
    up_part = up_weights
    gate_value = contract_last(portion, gate_part)
    up_value = contract_last(portion, up_part)
    hidden = (jax.nn.silu(gate_value) * up_value).astype(jnp.bfloat16)
    down_part = down_weights
    summed = lax.psum_scatter(
        contract_first(down_part, hidden).astype(jnp.bfloat16),
        "section",
        scatter_dimension=0,
        tiled=True,
    )
    expert_output = summed.reshape(feature_cols, expert_count, capacity)
    returned = lax.all_to_all(
        expert_output, "expert", split_axis=1, concat_axis=1, tiled=True
    ).reshape(feature_cols, slot_rows)
    forward_output = combine_rows(forward_mix, returned).astype(jnp.bfloat16)
    sent_grad = jnp.dot(
        backward_mix.T,
        output_grad.astype(jnp.float32),
        precision=lax.Precision.HIGHEST,
        preferred_element_type=jnp.float32,
    ).astype(jnp.bfloat16)
    arrived_grad = lax.all_to_all(
        sent_grad.reshape(expert_count, capacity, feature_cols),
        "expert",
        split_axis=0,
        concat_axis=0,
        tiled=True,
    )
    arrived_grad = arrived_grad.reshape(slot_rows, feature_cols)
    down_part = down_weights
    grad_hidden = contract_last(
        lax.all_gather(arrived_grad, "section", axis=1, tiled=True), down_part
    )
    gate_saved = gate_stash[0].astype(jnp.float32)
    up_saved = up_stash[0].astype(jnp.float32)
    sigmoid_gate = jax.nn.sigmoid(gate_saved)
    grad_gate = (
        grad_hidden * up_saved * sigmoid_gate * (1.0 + gate_saved * (1.0 - sigmoid_gate))
    ).astype(jnp.bfloat16)
    grad_up = (grad_hidden * gate_saved * sigmoid_gate).astype(jnp.bfloat16)
    gate_part = gate_weights
    up_part = up_weights
    summed_grad = lax.psum_scatter(
        (contract_first(gate_part, grad_gate) + contract_first(up_part, grad_up)).astype(
            jnp.bfloat16
        ),
        "section",
        scatter_dimension=0,
        tiled=True,
    )
    expert_grad = summed_grad.reshape(feature_cols, expert_count, capacity)
    returned_grad = lax.all_to_all(
        expert_grad, "expert", split_axis=1, concat_axis=1, tiled=True
    ).reshape(feature_cols, slot_rows)
    input_grad = combine_rows(backward_select, returned_grad).astype(jnp.bfloat16)
    return (forward_output, input_grad)


def solution(mesh):
    in_specs = (
        P("expert", "section"),
        P("expert", None),
        P("expert", None),
        P("expert", "section"),
        P("expert", None),
        P("expert", None),
        P("expert", None, "section"),
        P("expert", None, "section"),
        P("expert", "section", None),
        P("expert", "section", None),
        P("expert", "section", None),
    )
    out_specs = (P("expert", "section"), P("expert", "section"))
    return jax.shard_map(shards, mesh=mesh, in_specs=in_specs, out_specs=out_specs, check_vma=False)
```

profile of v0, /device:TPU:0, one launch (start us, length us, event | category | flops | bytes accessed | tf_op | source)
XLA Modules:
  0.0 145.0 jit_solution(15437782882217925766)
XLA Ops:
  7.2 0.0 copy-start
  7.2 0.0 copy-start.2
  7.2 0.8 convert_reduce_fusion.1
  8.0 1.0 select_reduce_fusion.1
  9.0 0.7 multiply_add_fusion
  9.7 0.8 select_reduce_fusion
  10.5 0.0 copy-done
  10.5 1.3 fusion.33
  11.8 7.4 %all-to-all-start.2 = ((bf16[16,8,1792]{2,1,0:T(8,128)(2,1)}), bf16[16,8,1792]{2,1,0:T(8,128)(2,1)S(1)}, u32[]{:S(2)}, u32[]{:S(2)}) async-start(bf16[16,8,1792]{2,1,0:T(8,128)(2,1)} %fusion.33), calls=%async_computation.3 | async-start | bytes 917504 | tf_op jit(solution)/shard_map/all_to_all | solution.py:109
  19.2 0.8 convert_reduce_fusion.3
  20.0 1.0 select_reduce_fusion.3
  21.0 0.7 multiply_add_fusion.1
  21.7 0.8 convert_reduce_fusion.2
  22.5 1.9 %fusion.34 = bf16[16,8,1792]{2,1,0:T(8,128)(2,1)} fusion(bf16[8,1792]{1,0:T(8,128)(2,1)} %param.11, bf16[8,128]{1,0:T(8,128)(2,1)S(1)} %get-tuple-element.4), kind=kOutput, calls=%fused_computation.22 | convolution fusion | flops 3899392 | bytes 489472 | tf_op jit(solution)/shard_map/dot_general | solution.py:74
  24.3 8.1 %all-to-all-done.2 = bf16[16,8,1792]{2,1,0:T(8,128)(2,1)S(1)} async-done(((bf16[16,8,1792]{2,1,0:T(8,128)(2,1)}), bf16[16,8,1792]{2,1,0:T(8,128)(2,1)S(1)}, u32[]{:S(2)}, u32[]{:S(2)}) %all-to-all-start.2) | async-done | bytes 458784 | tf_op jit(solution)/shard_map/all_to_all | solution.py:109
  32.5 3.9 %all-to-all-start = ((bf16[16,8,1792]{2,1,0:T(8,128)(2,1)}), bf16[16,8,1792]{2,1,0:T(8,128)(2,1)S(1)}, u32[]{:S(2)}, u32[]{:S(2)}) async-start(bf16[16,8,1792]{2,1,0:T(8,128)(2,1)} %fusion.34), calls=%async_computation | async-start | bytes 917504 | tf_op jit(solution)/shard_map/all_to_all | solution.py:77
  36.4 0.0 reduce-scatter.5.cloned.1.call-start
  36.4 0.0 copy-start.1
  36.4 13.7 %all_gather.7 = bf16[128,3584]{1,0:T(8,128)(2,1)S(1)} all-gather(bf16[128,1792]{1,0:T(8,128)(2,1)S(1)} %bitcast.76), channel_id=1, replica_groups=mesh['section'=2,'expert'=16] {'section'}, dimensions={1}, use_global_device_ids=true | all-gather | bytes 1376256 | tf_op jit(solution)/shard_map/all_gather | solution.py:119
  50.1 0.0 slice-start
  50.1 0.0 slice-start.1
  50.1 6.7 %fusion = f32[128,1280]{1,0:T(8,128)S(1)} fusion(bf16[128,3584]{1,0:T(8,128)(2,1)S(1)} %all_gather.7, bf16[1,1280,3584]{2,1,0:T(8,128)(2,1)} %param.21), kind=kOutput, calls=%fused_computation | convolution fusion | flops 1174405120 | bytes 10747904 | tf_op jit(solution)/shard_map/dot_general | solution.py:25
  56.8 0.0 copy-done.2
  56.8 0.0 copy-done.1
  56.8 0.0 slice-start.2
  56.9 0.0 copy-start.3
  56.9 1.4 fusion.4
  58.3 0.0 slice-done
  58.3 0.0 slice-done.1
  58.3 0.0 slice-done.2
  58.3 0.0 copy-done.3
  58.4 2.5 %fusion.24 = bf16[3584,128]{0,1:T(8,128)(2,1)} fusion(f32[128,3584]{1,0:T(8,128)S(1)} %fusion.4, bf16[1,1280,3584]{2,1,0:T(8,128)(2,1)S(1)} %bitcast.75, f32[128,1280]{1,0:T(8,128)S(1)} %fusion, bf16[1,128,1280]{2,1,0:T(8,128)(2,1)S(1)} %copy-done.3, bf16[1,128,1280]{2,1,0:T(8,128)(2,1)S(1)} %copy-done.2), kind=kOutput, calls=%fused_computation.16 | convolution fusion | flops 1177288704 | bytes 13238272 | tf_op jit(solution)/shard_map/dot_general | solution.py:31
  60.8 0.0 reduce-scatter.5.cloned.1.call-update
  60.9 0.0 reduce-scatter.3.cloned.1.call-start
  60.9 0.0 all-to-all-done
  60.9 17.9 %all_gather.6 = bf16[128,3584]{1,0:T(8,128)(2,1)S(1)} all-gather(bf16[128,1792]{1,0:T(8,128)(2,1)S(1)} %bitcast.77), channel_id=1, replica_groups=mesh['section'=2,'expert'=16] {'section'}, dimensions={1}, use_global_device_ids=true | all-gather | bytes 1376256 | tf_op jit(solution)/shard_map/all_gather | solution.py:85
  78.8 6.6 %fusion.10 = f32[128,1280]{1,0:T(8,128)S(1)} fusion(bf16[128,3584]{1,0:T(8,128)(2,1)S(1)} %all_gather.6, bf16[1,1280,3584]{2,1,0:T(8,128)(2,1)} %param.19), kind=kOutput, calls=%fused_computation.10 | convolution fusion | flops 1174405120 | bytes 10747904 | tf_op jit(solution)/shard_map/dot_general | solution.py:25
  85.4 12.3 %fusion.21 = bf16[3584,128]{0,1:T(8,128)(2,1)} fusion(bf16[1,1280,3584]{2,1,0:T(8,128)(2,1)} %param.21, bf16[128,3584]{1,0:T(8,128)(2,1)S(1)} %all_gather.6, bf16[1,1280,3584]{2,1,0:T(8,128)(2,1)} %param.20, f32[128,1280]{1,0:T(8,128)S(1)} %fusion.10), kind=kOutput, calls=%fused_computation.15 | convolution fusion | flops 2350252032 | bytes 20840448 | tf_op jit(solution)/shard_map/dot_general | solution.py:31
  97.7 0.0 reduce-scatter.3.cloned.1.call-update
  97.8 0.0 reduce-scatter.5.cloned.1.call-done
  97.8 5.3 %all-to-all-start.3 = ((bf16[1792,16,8]{0,2,1:T(8,128)(2,1)}), bf16[1792,16,8]{0,2,1:T(8,128)(2,1)S(1)}, u32[]{:S(2)}, u32[]{:S(2)}) async-start(bf16[1792,16,8]{0,2,1:T(8,128)(2,1)} %bitcast.78), calls=%async_computation.5 | async-start | bytes 917504 | tf_op jit(solution)/shard_map/all_to_all | solution.py:139
  103.1 15.3 %reduce-scatter.3.cloned.1.call-done = bf16[1792,128]{0,1:T(8,128)(2,1)} async-done(((bf16[3584,128]{0,1:T(8,128)(2,1)}), bf16[1792,128]{0,1:T(8,128)(2,1)}) %reduce-scatter.3.cloned.1.call-update) | async-done | bytes 458768 | tf_op jit(solution)/shard_map/reduce_scatter | solution.py:92
  118.4 0.0 all-to-all-done.3
  118.4 5.6 %all-to-all-start.1 = ((bf16[1792,16,8]{0,2,1:T(8,128)(2,1)}), bf16[1792,16,8]{0,2,1:T(8,128)(2,1)S(1)}, u32[]{:S(2)}, u32[]{:S(2)}) async-start(bf16[1792,16,8]{0,2,1:T(8,128)(2,1)} %bitcast.79), calls=%async_computation.2 | async-start | bytes 917504 | tf_op jit(solution)/shard_map/all_to_all | solution.py:99
  124.0 0.9 convolution_convert_fusion.2
  124.9 12.3 %all-to-all-done.1 = bf16[1792,16,8]{0,2,1:T(8,128)(2,1)S(1)} async-done(((bf16[1792,16,8]{0,2,1:T(8,128)(2,1)}), bf16[1792,16,8]{0,2,1:T(8,128)(2,1)S(1)}, u32[]{:S(2)}, u32[]{:S(2)}) %all-to-all-start.1) | async-done | bytes 458784 | tf_op jit(solution)/shard_map/all_to_all | solution.py:99
  137.3 0.9 convolution_convert_fusion.3
  (5 shorter events, 0.1 us)
Async XLA Ops:
  7.2 3.3 %copy-start = (bf16[8,1792]{1,0:T(8,128)(2,1)S(1)}, bf16[8,1792]{1,0:T(8,128)(2,1)}, u32[]{:S(2)}) copy-start(bf16[8,1792]{1,0:T(8,128)(2,1)} %param.14) | copy-start | bytes 86020
  7.2 49.6 %copy-start.2 = (bf16[1,128,1280]{2,1,0:T(8,128)(2,1)S(1)}, bf16[1,128,1280]{2,1,0:T(8,128)(2,1)}, u32[]{:S(2)}) copy-start(bf16[1,128,1280]{2,1,0:T(8,128)(2,1)} %param.17) | copy-start | bytes 983044
  11.8 20.6 %all-to-all-start.2 = ((bf16[16,8,1792]{2,1,0:T(8,128)(2,1)}), bf16[16,8,1792]{2,1,0:T(8,128)(2,1)S(1)}, u32[]{:S(2)}, u32[]{:S(2)}) async-start(bf16[16,8,1792]{2,1,0:T(8,128)(2,1)} %fusion.33), calls=%async_computation.3 | async-start | bytes 917504 | tf_op jit(solution)/shard_map/all_to_all | solution.py:109
  32.5 28.5 %all-to-all-start = ((bf16[16,8,1792]{2,1,0:T(8,128)(2,1)}), bf16[16,8,1792]{2,1,0:T(8,128)(2,1)S(1)}, u32[]{:S(2)}, u32[]{:S(2)}) async-start(bf16[16,8,1792]{2,1,0:T(8,128)(2,1)} %fusion.34), calls=%async_computation | async-start | bytes 917504 | tf_op jit(solution)/shard_map/all_to_all | solution.py:77
  36.4 61.4 %reduce-scatter.5.cloned.1.call-start = ((), (), s32[]{:S(2)}) async-start(), calls=%async_computation.7 | async-start | bytes 1376256 | tf_op jit(solution)/shard_map/reduce_scatter | solution.py:130
  36.4 20.4 %copy-start.1 = (bf16[1,1280,3584]{2,1,0:T(8,128)(2,1)S(1)}, bf16[1,1280,3584]{2,1,0:T(8,128)(2,1)}, u32[]{:S(2)}) copy-start(bf16[1,1280,3584]{2,1,0:T(8,128)(2,1)} %param.20) | copy-start | bytes 27525124
  50.1 8.2 %slice-start = ((s8[9175040]{0:T(1024)(128)(4,1)}), s8[4194304]{0:T(1024)(128)(4,1)S(1)}, s32[]{:S(2)}) async-start(s8[9175040]{0:T(1024)(128)(4,1)} %bitcast.74), calls=%async_computation.8 | async-start | bytes 8388608
  50.1 8.2 %slice-start.1 = ((s8[9175040]{0:T(1024)(128)(4,1)}), s8[4194304]{0:T(1024)(128)(4,1)S(1)}, s32[]{:S(2)}) async-start(s8[9175040]{0:T(1024)(128)(4,1)} %bitcast.74), calls=%async_computation.9 | async-start | bytes 8388608
  56.8 1.5 %slice-start.2 = ((s8[9175040]{0:T(1024)(128)(4,1)}), s8[786432]{0:T(1024)(128)(4,1)S(1)}, s32[]{:S(2)}) async-start(s8[9175040]{0:T(1024)(128)(4,1)} %bitcast.74), calls=%async_computation.10 | async-start | bytes 1572864
  56.9 1.5 %copy-start.3 = (bf16[1,128,1280]{2,1,0:T(8,128)(2,1)S(1)}, bf16[1,128,1280]{2,1,0:T(8,128)(2,1)}, u32[]{:S(2)}) copy-start(bf16[1,128,1280]{2,1,0:T(8,128)(2,1)} %param.18) | copy-start | bytes 983044
  60.9 57.5 %reduce-scatter.3.cloned.1.call-start = ((), (), s32[]{:S(2)}) async-start(), calls=%async_computation.6 | async-start | bytes 1376256 | tf_op jit(solution)/shard_map/reduce_scatter | solution.py:92
  97.8 20.6 %all-to-all-start.3 = ((bf16[1792,16,8]{0,2,1:T(8,128)(2,1)}), bf16[1792,16,8]{0,2,1:T(8,128)(2,1)S(1)}, u32[]{:S(2)}, u32[]{:S(2)}) async-start(bf16[1792,16,8]{0,2,1:T(8,128)(2,1)} %bitcast.78), calls=%async_computation.5 | async-start | bytes 917504 | tf_op jit(solution)/shard_map/all_to_all | solution.py:139
  118.4 18.9 %all-to-all-start.1 = ((bf16[1792,16,8]{0,2,1:T(8,128)(2,1)}), bf16[1792,16,8]{0,2,1:T(8,128)(2,1)S(1)}, u32[]{:S(2)}, u32[]{:S(2)}) async-start(bf16[1792,16,8]{0,2,1:T(8,128)(2,1)} %bitcast.79), calls=%async_computation.2 | async-start | bytes 917504 | tf_op jit(solution)/shard_map/all_to_all | solution.py:99
Sparse Core Ops, SparseCore 0:
  61.0 23.5 reduce-scatter.4
  97.9 20.4 reduce-scatter.2
where the time goes:
time: 146 us; the launch traced here: 145 us
  waiting for transfers between devices  35.8 us (25%)
  matrix products  34.6 us (24%)
  blocking collectives  31.5 us (22%)
  starting transfers between devices  22.2 us (15%)
  between operations  14.3 us (10%)
  other arithmetic  6.52 us (4%)
    all_gather x1, blocking collectives, shards(): portion = lax.all_gather(arrived, 'section', axis=1, tiled=True)  17.9 us
    dot_general x3, matrix products, contract_first(): lax.dot_general(first_operand, second_operand, (((0,), (1,)), ((), ())),...  16.2 us
    reduce_scatter x1, waiting for transfers between devices, shards(): lax.psum_scatter(contract_first(down_part, hidden).astype(jnp.bfloat16),...  15.3 us
    all_gather x1, blocking collectives, shards(): lax.all_gather(arrived_grad, 'section', axis=1, tiled=True)  13.7 us
    dot_general x2, matrix products, contract_last(): lax.dot_general(first_operand, second_operand, (((1,), (1,)), ((), ())),...  13.3 us
    all_to_all x1, waiting for transfers between devices, shards(): lax.all_to_all(expert_output, 'expert', split_axis=1, concat_axis=1, tile...  12.3 us
    all_to_all x1, waiting for transfers between devices, shards(): lax.all_to_all(sent_grad.reshape(expert_count, capacity, feature_cols), '...  8.14 us
    all_to_all x1, starting transfers between devices, shards(): lax.all_to_all(sent_grad.reshape(expert_count, capacity, feature_cols), '...  7.36 us
  transfers between devices with their start and end apart: 6, of which 3 were waited for; matrix products, arithmetic and copies ran while one was open for 25% of the time, Pallas kernels for 0%

commit v1 on v0

--- a/solution.py
+++ b/solution.py
@@ -96,8 +96,11 @@
         tiled=True,
     )
     expert_output = summed.reshape(feature_cols, expert_count, capacity)
-    returned = lax.all_to_all(
-        expert_output, "expert", split_axis=1, concat_axis=1, tiled=True
+    returned = jnp.concatenate(
+        lax.all_to_all(
+            jnp.stack(jnp.split(expert_output, lax.axis_size("expert"), axis=1)), "expert", 0, 0
+        ),
+        axis=1,
     ).reshape(feature_cols, slot_rows)
     forward_output = combine_rows(forward_mix, returned).astype(jnp.bfloat16)
     sent_grad = jnp.dot(

time: 146 us -> 169 us (1.16)
  local copies, waits for them, and re-layouts: 0.04 us -> 21.7 us
  blocking collectives: 31.5 us -> 26.4 us
  matrix products: 34.6 us -> 38.3 us
  waiting for transfers between devices: 35.8 us -> 38.6 us
    unnamed x14 -> x27, local copies, waits for them, and re-layouts: 0.04 us -> 20.4 us
    all_to_all x1, waiting for transfers between devices: 0.01 us -> 12.3 us  [shards(): lax.all_to_all(expert_grad, 'expert', split_axis=1, concat_axis=1, tiled=...]
    reduce_scatter x1, waiting for transfers between devices: 15.3 us -> 5.05 us  [shards(): lax.psum_scatter(contract_first(down_part, hidden).astype(jnp.bfloat16),...]
    all_to_all x1, waiting for transfers between devices: 8.14 us -> 0.01 us  [shards(): lax.all_to_all(sent_grad.reshape(expert_count, capacity, feature_cols), '...]
    all_to_all x1, waiting for transfers between devices: 0.01 us -> 7.89 us  [shards(): lax.all_to_all(sent.reshape(expert_count, capacity, feature_cols), 'exper...]
    all_gather x1, blocking collectives: 17.9 us -> 13.5 us  [shards(): portion = lax.all_gather(arrived, 'section', axis=1, tiled=True)]
    dot_general x3, matrix products: 16.2 us -> 20 us  [contract_first(): lax.dot_general(first_operand, second_operand, (((0,), (1,)), ((), ())),...]
    all_to_all x1, starting transfers between devices: 7.36 us -> 3.89 us  [shards(): lax.all_to_all(sent_grad.reshape(expert_count, capacity, feature_cols), '...]
  transfers between devices with their start and end apart: 6 -> 6, of which waited for: 3 -> 4; matrix products, arithmetic and copies ran while one was open for 25% -> 25% of each run, Pallas kernels for 0% -> 0%
where the time goes in v1:
time: 169 us; the launch traced here: 167 us
  waiting for transfers between devices  38.6 us (23%)
  matrix products  38.3 us (23%)
  blocking collectives  26.4 us (16%)
  local copies, waits for them, and re-layouts  21.7 us (13%)
  starting transfers between devices  20.9 us (12%)
  between operations  14.2 us (8%)
  other arithmetic  6.48 us (4%)
    unnamed x27, local copies, waits for them, and re-layouts  20.4 us
    dot_general x3, matrix products, contract_first(): lax.dot_general(first_operand, second_operand, (((0,), (1,)), ((), ())),...  20 us
    all_gather x1, blocking collectives, shards(): portion = lax.all_gather(arrived, 'section', axis=1, tiled=True)  13.5 us
    dot_general x2, matrix products, contract_last(): lax.dot_general(first_operand, second_operand, (((1,), (1,)), ((), ())),...  13.3 us
    all_to_all x1, waiting for transfers between devices, shards(): lax.all_to_all(jnp.stack(jnp.split(expert_output, lax.axis_size('expert')...  13.2 us
    all_gather x1, blocking collectives, shards(): lax.all_gather(arrived_grad, 'section', axis=1, tiled=True)  12.9 us
    all_to_all x1, waiting for transfers between devices, shards(): lax.all_to_all(expert_grad, 'expert', split_axis=1, concat_axis=1, tiled=...  12.3 us
    all_to_all x1, waiting for transfers between devices, shards(): lax.all_to_all(sent.reshape(expert_count, capacity, feature_cols), 'exper...  7.89 us
  transfers between devices with their start and end apart: 6, of which 4 were waited for; matrix products, arithmetic and copies ran while one was open for 25% of the time, Pallas kernels for 0%

profile of v1, /device:TPU:0, one launch (start us, length us, event | category | flops | bytes accessed | tf_op | source)
XLA Modules:
  0.0 166.6 jit_solution(5427254756981021280)
XLA Ops:
  7.2 0.8 convert_reduce_fusion.3
  8.0 1.0 select_reduce_fusion.3
  9.0 0.7 multiply_add_fusion.1
  9.7 0.8 convert_reduce_fusion.2
  10.4 1.1 fusion.34
  11.5 7.4 %all-to-all-start = ((bf16[16,8,1792]{2,1,0:T(8,128)(2,1)}), bf16[16,8,1792]{2,1,0:T(8,128)(2,1)S(1)}, u32[]{:S(2)}, u32[]{:S(2)}) async-start(bf16[16,8,1792]{2,1,0:T(8,128)(2,1)} %fusion.34), calls=%async_computation | async-start | bytes 917504 | tf_op jit(solution)/shard_map/all_to_all | solution.py:77
  18.9 0.8 convert_reduce_fusion.1
  19.7 1.0 select_reduce_fusion.1
  20.7 0.7 multiply_add_fusion
  21.4 0.8 select_reduce_fusion
  22.2 2.1 %fusion.33 = bf16[16,8,1792]{2,1,0:T(8,128)(2,1)} fusion(f32[8,128]{1,0:T(8,128)S(1)} %get-tuple-element.2, bf16[8,1792]{1,0:T(8,128)(2,1)} %param.14), kind=kOutput, calls=%fused_computation.21 | convolution fusion | flops 22249472 | bytes 491520 | tf_op jit(solution)/shard_map/dot_general | solution.py:106
  24.3 7.9 %all-to-all-done = bf16[16,8,1792]{2,1,0:T(8,128)(2,1)S(1)} async-done(((bf16[16,8,1792]{2,1,0:T(8,128)(2,1)}), bf16[16,8,1792]{2,1,0:T(8,128)(2,1)S(1)}, u32[]{:S(2)}, u32[]{:S(2)}) %all-to-all-start) | async-done | bytes 458784 | tf_op jit(solution)/shard_map/all_to_all | solution.py:77
  32.2 3.9 %all-to-all-start.2 = ((bf16[16,8,1792]{2,1,0:T(8,128)(2,1)}), bf16[16,8,1792]{2,1,0:T(8,128)(2,1)S(1)}, u32[]{:S(2)}, u32[]{:S(2)}) async-start(bf16[16,8,1792]{2,1,0:T(8,128)(2,1)} %fusion.33), calls=%async_computation.3 | async-start | bytes 917504 | tf_op jit(solution)/shard_map/all_to_all | solution.py:112
  36.1 0.0 reduce-scatter.3.cloned.1.call-start
  36.1 13.5 %all_gather.6 = bf16[128,3584]{1,0:T(8,128)(2,1)S(1)} all-gather(bf16[128,1792]{1,0:T(8,128)(2,1)S(1)} %bitcast.142), channel_id=1, replica_groups=mesh['section'=2,'expert'=16] {'section'}, dimensions={1}, use_global_device_ids=true | all-gather | bytes 1376256 | tf_op jit(solution)/shard_map/all_gather | solution.py:85
  49.7 12.9 %all_gather.7 = bf16[128,3584]{1,0:T(8,128)(2,1)S(1)} all-gather(bf16[128,1792]{1,0:T(8,128)(2,1)S(1)} %bitcast.143), channel_id=1, replica_groups=mesh['section'=2,'expert'=16] {'section'}, dimensions={1}, use_global_device_ids=true | all-gather | bytes 1376256 | tf_op jit(solution)/shard_map/all_gather | solution.py:122
  62.5 6.6 %fusion.10 = f32[128,1280]{1,0:T(8,128)S(1)} fusion(bf16[128,3584]{1,0:T(8,128)(2,1)S(1)} %all_gather.6, bf16[1,1280,3584]{2,1,0:T(8,128)(2,1)} %param.19), kind=kOutput, calls=%fused_computation.10 | convolution fusion | flops 1174405120 | bytes 10747904 | tf_op jit(solution)/shard_map/dot_general | solution.py:25
  69.1 12.3 %fusion.21 = bf16[3584,128]{0,1:T(8,128)(2,1)} fusion(bf16[1,1280,3584]{2,1,0:T(8,128)(2,1)} %param.21, bf16[128,3584]{1,0:T(8,128)(2,1)S(1)} %all_gather.6, bf16[1,1280,3584]{2,1,0:T(8,128)(2,1)} %param.20, f32[128,1280]{1,0:T(8,128)S(1)} %fusion.10), kind=kOutput, calls=%fused_computation.15 | convolution fusion | flops 2350252032 | bytes 20840448 | tf_op jit(solution)/shard_map/dot_general | solution.py:31
  81.4 0.0 reduce-scatter.3.cloned.1.call-update
  81.5 0.0 reduce-scatter.5.cloned.1.call-start
  81.5 6.7 %fusion = f32[128,1280]{1,0:T(8,128)S(1)} fusion(bf16[128,3584]{1,0:T(8,128)(2,1)S(1)} %all_gather.7, bf16[1,1280,3584]{2,1,0:T(8,128)(2,1)} %param.21), kind=kOutput, calls=%fused_computation | convolution fusion | flops 1174405120 | bytes 10747904 | tf_op jit(solution)/shard_map/dot_general | solution.py:25
  88.3 5.2 %fusion.4 = f32[128,3584]{1,0:T(8,128)S(1)} fusion(bf16[1,1280,3584]{2,1,0:T(8,128)(2,1)} %param.20, f32[128,1280]{1,0:T(8,128)S(1)} %fusion, bf16[1,128,1280]{2,1,0:T(8,128)(2,1)S(1)} %copy-done.1), kind=kOutput, calls=%fused_computation.4 | convolution fusion | flops 1175552000 | bytes 11993088 | tf_op jit(solution)/shard_map/dot_general | solution.py:31
  93.5 2.5 %fusion.24 = bf16[3584,128]{0,1:T(8,128)(2,1)} fusion(f32[128,3584]{1,0:T(8,128)S(1)} %fusion.4, bf16[1,1280,3584]{2,1,0:T(8,128)(2,1)S(1)} %bitcast.141, f32[128,1280]{1,0:T(8,128)S(1)} %fusion, bf16[1,128,1280]{2,1,0:T(8,128)(2,1)S(1)} %copy-done.2, bf16[1,128,1280]{2,1,0:T(8,128)(2,1)S(1)} %copy-done.1), kind=kOutput, calls=%fused_computation.16 | convolution fusion | flops 1177288704 | bytes 13238272 | tf_op jit(solution)/shard_map/dot_general | solution.py:31
  96.0 0.0 reduce-scatter.5.cloned.1.call-update
  96.0 5.0 %reduce-scatter.3.cloned.1.call-done = bf16[1792,128]{0,1:T(8,128)(2,1)} async-done(((bf16[3584,128]{0,1:T(8,128)(2,1)}), bf16[1792,128]{0,1:T(8,128)(2,1)}) %reduce-scatter.3.cloned.1.call-update) | async-done | bytes 458768 | tf_op jit(solution)/shard_map/reduce_scatter | solution.py:92
  101.1 1.3 constant_dynamic-update-slice_fusion.15
  102.4 1.3 constant_dynamic-update-slice_fusion.14
  103.8 1.4 constant_dynamic-update-slice_fusion.13
  105.1 1.4 constant_dynamic-update-slice_fusion.12
  106.5 1.4 constant_dynamic-update-slice_fusion.11
  107.9 1.4 constant_dynamic-update-slice_fusion.10
  109.2 1.4 constant_dynamic-update-slice_fusion.9
  110.6 1.3 constant_dynamic-update-slice_fusion.8
  111.9 1.4 constant_dynamic-update-slice_fusion.7
  113.3 1.4 constant_dynamic-update-slice_fusion.6
  114.6 1.4 constant_dynamic-update-slice_fusion.5
  116.0 1.4 constant_dynamic-update-slice_fusion.4
  117.3 1.4 constant_dynamic-update-slice_fusion.3
  118.7 1.4 constant_dynamic-update-slice_fusion.2
  120.1 1.3 constant_dynamic-update-slice_fusion.1
  121.4 1.3 constant_dynamic-update-slice_fusion
  122.8 5.6 %all-to-all-start.1 = ((bf16[16,1792,1,8]{1,3,2,0:T(8,128)(2,1)}), bf16[16,1792,1,8]{1,3,2,0:T(8,128)(2,1)S(1)}, u32[]{:S(2)}, u32[]{:S(2)}) async-start(bf16[16,1792,1,8]{1,3,2,0:T(8,128)(2,1)} %constant_dynamic-update-slice_fusion), calls=%async_computation.2 | async-start | bytes 917504 | tf_op jit(solution)/shard_map/all_to_all | solution.py:100
  128.4 0.0 reduce-scatter.5.cloned.1.call-done
  128.4 13.2 %all-to-all-done.1 = bf16[16,1792,1,8]{1,3,2,0:T(8,128)(2,1)S(1)} async-done(((bf16[16,1792,1,8]{1,3,2,0:T(8,128)(2,1)}), bf16[16,1792,1,8]{1,3,2,0:T(8,128)(2,1)S(1)}, u32[]{:S(2)}, u32[]{:S(2)}) %all-to-all-start.1) | async-done | bytes 458784 | tf_op jit(solution)/shard_map/all_to_all | solution.py:100
  141.7 3.9 %all-to-all-start.3 = ((bf16[1792,16,8]{0,2,1:T(8,128)(2,1)}), bf16[1792,16,8]{0,2,1:T(8,128)(2,1)S(1)}, u32[]{:S(2)}, u32[]{:S(2)}) async-start(bf16[1792,16,8]{0,2,1:T(8,128)(2,1)} %bitcast.144), calls=%async_computation.5 | async-start | bytes 917504 | tf_op jit(solution)/shard_map/all_to_all | solution.py:142
  145.6 0.9 convolution_convert_fusion.3
  146.5 12.3 %all-to-all-done.3 = bf16[1792,16,8]{0,2,1:T(8,128)(2,1)S(1)} async-done(((bf16[1792,16,8]{0,2,1:T(8,128)(2,1)}), bf16[1792,16,8]{0,2,1:T(8,128)(2,1)S(1)}, u32[]{:S(2)}, u32[]{:S(2)}) %all-to-all-start.3) | async-done | bytes 458784 | tf_op jit(solution)/shard_map/all_to_all | solution.py:142
  158.8 0.9 convolution_convert_fusion.2
  (18 shorter events, 0.1 us)
Async XLA Ops:
  7.2 3.3 %copy-start = (bf16[8,1792]{1,0:T(8,128)(2,1)S(1)}, bf16[8,1792]{1,0:T(8,128)(2,1)}, u32[]{:S(2)}) copy-start(bf16[8,1792]{1,0:T(8,128)(2,1)} %param.11) | copy-start | bytes 86020
  11.5 20.6 %all-to-all-start = ((bf16[16,8,1792]{2,1,0:T(8,128)(2,1)}), bf16[16,8,1792]{2,1,0:T(8,128)(2,1)S(1)}, u32[]{:S(2)}, u32[]{:S(2)}) async-start(bf16[16,8,1792]{2,1,0:T(8,128)(2,1)} %fusion.34), calls=%async_computation | async-start | bytes 917504 | tf_op jit(solution)/shard_map/all_to_all | solution.py:77
  32.2 17.5 %all-to-all-start.2 = ((bf16[16,8,1792]{2,1,0:T(8,128)(2,1)}), bf16[16,8,1792]{2,1,0:T(8,128)(2,1)S(1)}, u32[]{:S(2)}, u32[]{:S(2)}) async-start(bf16[16,8,1792]{2,1,0:T(8,128)(2,1)} %fusion.33), calls=%async_computation.3 | async-start | bytes 917504 | tf_op jit(solution)/shard_map/all_to_all | solution.py:112
  36.1 65.0 %reduce-scatter.3.cloned.1.call-start = ((), (), s32[]{:S(2)}) async-start(), calls=%async_computation.6 | async-start | bytes 1376256 | tf_op jit(solution)/shard_map/reduce_scatter | solution.py:92
  81.4 6.8 %copy-start.1 = (bf16[1,128,1280]{2,1,0:T(8,128)(2,1)S(1)}, bf16[1,128,1280]{2,1,0:T(8,128)(2,1)}, u32[]{:S(2)}) copy-start(bf16[1,128,1280]{2,1,0:T(8,128)(2,1)} %param.17) | copy-start | bytes 983044
  81.5 47.0 %reduce-scatter.5.cloned.1.call-start = ((), (), s32[]{:S(2)}) async-start(), calls=%async_computation.7 | async-start | bytes 1376256 | tf_op jit(solution)/shard_map/reduce_scatter | solution.py:133
  81.5 12.0 %slice-start = ((s8[9175040]{0:T(1024)(128)(4,1)}), s8[4194304]{0:T(1024)(128)(4,1)S(1)}, s32[]{:S(2)}) async-start(s8[9175040]{0:T(1024)(128)(4,1)} %bitcast.140), calls=%async_computation.8 | async-start | bytes 8388608
  81.5 12.0 %slice-start.1 = ((s8[9175040]{0:T(1024)(128)(4,1)}), s8[786432]{0:T(1024)(128)(4,1)S(1)}, s32[]{:S(2)}) async-start(s8[9175040]{0:T(1024)(128)(4,1)} %bitcast.140), calls=%async_computation.9 | async-start | bytes 1572864
  88.3 5.2 %slice-start.2 = ((s8[9175040]{0:T(1024)(128)(4,1)}), s8[4194304]{0:T(1024)(128)(4,1)S(1)}, s32[]{:S(2)}) async-start(s8[9175040]{0:T(1024)(128)(4,1)} %bitcast.140), calls=%async_computation.10 | async-start | bytes 8388608
  88.3 5.2 %copy-start.2 = (bf16[1,128,1280]{2,1,0:T(8,128)(2,1)S(1)}, bf16[1,128,1280]{2,1,0:T(8,128)(2,1)}, u32[]{:S(2)}) copy-start(bf16[1,128,1280]{2,1,0:T(8,128)(2,1)} %param.18) | copy-start | bytes 983044
  122.8 18.9 %all-to-all-start.1 = ((bf16[16,1792,1,8]{1,3,2,0:T(8,128)(2,1)}), bf16[16,1792,1,8]{1,3,2,0:T(8,128)(2,1)S(1)}, u32[]{:S(2)}, u32[]{:S(2)}) async-start(bf16[16,1792,1,8]{1,3,2,0:T(8,128)(2,1)} %constant_dynamic-update-slice_fusion), calls=%async_computation.2 | async-start | bytes 917504 | tf_op jit(solution)/shard_map/all_to_all | solution.py:100
  141.7 17.2 %all-to-all-start.3 = ((bf16[1792,16,8]{0,2,1:T(8,128)(2,1)}), bf16[1792,16,8]{0,2,1:T(8,128)(2,1)S(1)}, u32[]{:S(2)}, u32[]{:S(2)}) async-start(bf16[1792,16,8]{0,2,1:T(8,128)(2,1)} %bitcast.144), calls=%async_computation.5 | async-start | bytes 917504 | tf_op jit(solution)/shard_map/all_to_all | solution.py:142
Sparse Core Ops, SparseCore 0:
  81.6 19.4 reduce-scatter.2
  103.4 18.8 reduce-scatter.4
